TPU v7x, 32 devices: a whole 2x2x4 slice. The times are simulated.
32 devices in a mesh: rows: 8 (over z, core), ch: 4 (over y, x).
Axes of the slice: x: 2, y: 2, z: 4, core: 2. Of those that a mesh axis runs over, the one named last changes fastest.
Arguments:
- features: bfloat16 [32, 256, 2048], P('rows', None, 'ch'), may hold values from -6 to 6
- conv_weight: bfloat16 [3, 3, 256, 256], P(None, None, 'ch'), may hold values from -0.125 to 0.125
- cotangent: bfloat16 [32, 256, 2048], P('rows', None, 'ch'), may hold values from -6 to 6
- valid_rows: int32 [16], replicated, may hold values from 16 to 32
Outputs:
- input_grad: bfloat16 [32, 256, 2048], P('rows', None, 'ch')
- weight_grad: float32 [3, 3, 256, 256], P(None, None, 'ch')
All inputs are finite; a program needn't handle non-finite values.
Results may differ from a plain program's by a relative error of at most 0.0049.
Values may be sent and summed in bfloat16 or wider, within the bound.
A program may use at most 64 MiB of HBM per device.

v0:
```python
import jax
import jax.numpy as jnp
from jax import lax
from jax.sharding import PartitionSpec as P

COLS = 128


def padded_2(block, sides, width):
    for axis, dim in sides:
        count = lax.axis_size(axis)
        forward = [(i, i + 1) for i in range(count - 1)]
        backward = [(target, source) for source, target in forward]
        low = lax.ppermute(
            lax.slice_in_dim(block, block.shape[dim] - width, None, axis=dim), axis, forward
        )
        high = lax.ppermute(lax.slice_in_dim(block, 0, width, axis=dim), axis, backward)
        block = jnp.concatenate([low, block, high], axis=dim)
    return block


def shift_cols(field, across, columns):
    if across == 0:
        return field
    length = field.shape[-1]
    widths = [(0, 0)] * (field.ndim - 1) + [(1, 1)]
    padded = jnp.pad(field, widths)
    moved = padded[..., 1 + across : 1 + across + length]
    position = jnp.arange(length).astype(jnp.int32) % columns + across
    inside = (position >= 0) & (position < columns)
    return jnp.where(inside, moved, jnp.zeros_like(moved))


def body(features, conv_weight, cotangent, valid_rows):
    band = features.shape[0]
    total_ch = features.shape[1]
    cells = features.shape[2]
    columns = COLS
    img_count = cells // columns
    kernel = lax.all_gather(conv_weight, "ch", axis=2, tiled=True)
    padded = padded_2(features, (("rows", 0),), 1)
    summed = jnp.zeros(features.shape, jnp.float32)
    for offset_row in range(3):
        for offset_col in range(3):
            window = shift_cols(padded[offset_row : offset_row + band], offset_col - 1, columns)
            summed = summed + jnp.einsum(
                "hik,oi->hok",
                window,
                kernel[offset_row, offset_col],
                preferred_element_type=jnp.float32,
            )
    center = jnp.sum(summed, 1) / total_ch
    inverse = lax.rsqrt(jnp.sum(summed * summed, 1) / total_ch - center * center + 1e-06)
    normed = (summed - center[:, None, :]) * inverse[:, None, :]
    row_ids = lax.axis_index("rows") * band + jnp.arange(band)
    local_limits = lax.dynamic_slice_in_dim(
        valid_rows, lax.axis_index("ch") * img_count, img_count, 0
    )
    limits = jnp.repeat(local_limits, columns, total_repeat_length=cells)
    keep = (row_ids[:, None] < limits[None, :]).astype(jnp.float32)
    masked = cotangent.astype(jnp.float32) * keep[:, None, :]
    grad_total = jnp.sum(masked, 1)
    grad_cross = jnp.sum(masked * normed, 1)
    grad_pre = (
        inverse[:, None, :]
        * (
            masked
            - (grad_total / total_ch)[:, None, :]
            - normed * (grad_cross / total_ch)[:, None, :]
        )
    ).astype(jnp.bfloat16)
    taps = []
    for offset_row in range(3):
        for offset_col in range(3):
            window = shift_cols(padded[offset_row : offset_row + band], offset_col - 1, columns)
            taps.append(
                jnp.einsum("hik,hok->oi", window, grad_pre, preferred_element_type=jnp.float32)
            )
    weight_part = jnp.stack(taps).reshape((3, 3, total_ch, total_ch))
    share = lax.psum_scatter(weight_part, "ch", scatter_dimension=2, tiled=True)
    weight_grad = lax.psum(share, "rows")
    grad_padded = padded_2(grad_pre, (("rows", 0),), 1)
    input_sum = jnp.zeros(features.shape, jnp.float32)
    for offset_row in range(3):
        for offset_col in range(3):
            window = shift_cols(
                grad_padded[2 - offset_row : 2 - offset_row + band], 1 - offset_col, columns
            )
            input_sum = input_sum + jnp.einsum(
                "hok,oi->hik",
                window,
                kernel[offset_row, offset_col],
                preferred_element_type=jnp.float32,
            )
    return (input_sum.astype(jnp.bfloat16), weight_grad)


def solution(mesh):
    in_specs = (P("rows", None, "ch"), P(None, None, "ch", None), P("rows", None, "ch"), P())
    out_specs = (P("rows", None, "ch"), P(None, None, "ch", None))
    return jax.shard_map(body, mesh=mesh, in_specs=in_specs, out_specs=out_specs, check_vma=False)
```

profile of v0, /device:TPU:0, one launch (start us, length us, event | category | flops | bytes accessed | tf_op | source)
XLA Modules:
  0.0 162.9 jit_solution(7668742994701434152)
XLA Ops:
  7.2 0.7 all-gather.2.cloned.1.call-update
  8.0 1.5 copy.6
  9.5 2.4 %collective-permute-start = (bf16[1,256,512]{1,2,0:T(8,128)(2,1)S(1)}, bf16[1,256,512]{1,2,0:T(8,128)(2,1)S(1)}, u32[]{:S(2)}, u32[]{:S(2)}) collective-permute-start(bf16[1,256,512]{1,2,0:T(8,128)(2,1)S(1)} %get-tuple-element.26), channel_id=1, source_target_pairs={{0,4},{4,8},{8,12},{12,16},{16,20},{20,24},{24,28},{1,5},{5,9},{9,... | collective-permute-start | bytes 786440 | tf_op jit(solution)/shard_map/ppermute | solution.py:14
  11.9 1.3 collective-permute-start.1
  13.3 0.7 fusion.92
  14.0 2.6 %compare_select_fusion.1 = s32[512,1]{0,1:T(1,128)S(1)} fusion(s32[512,1]{0,1:T(1,128)S(1)} %bitcast.155, s32[512,1]{0,1:T(1,128)S(1)} %bitcast.154, s32[]{:T(128)} %bitcast.28, s32[]{:T(128)} %bitcast.29, s32[]{:T(128)} %bitcast.31, s32[]{:T(128)} %bitcast.30), kind=kLoop, calls=%fused_computation.107 | loop fusion | flops 4096 | bytes 6160 | tf_op jit(solution)/shard_map/jit(_take)/gather | solution.py:59
  16.6 1.3 copy.12
  18.0 0.7 copy-done.7
  18.7 1.1 pad_maximum_fusion.1
  19.8 20.3 %all-gather.2.cloned.1.call-done = bf16[3,3,256,256]{3,2,1,0:T(8,128)(2,1)} async-done(((bf16[3,3,64,256]{3,2,1,0:T(8,128)(2,1)}), bf16[3,3,256,256]{3,2,1,0:T(8,128)(2,1)}) %all-gather.2.cloned.1.call-update) | async-done | bytes 1179664 | tf_op jit(solution)/shard_map/all_gather | solution.py:40
  40.2 1.5 fusion.53
  41.7 0.5 fusion.54
  42.2 0.5 fusion.57
  42.7 0.5 fusion.58
  43.2 0.4 copy-done.8
  43.6 0.5 fusion.3
  44.1 0.5 fusion.55
  44.6 0.5 fusion.56
  45.1 0.7 copy-done.2
  45.8 0.6 fusion.60
  46.4 1.4 multiply_reduce_fusion.1
  47.8 1.6 fusion.1
  49.4 1.7 %multiply_convert_fusion = bf16[4,256,512]{1,2,0:T(8,128)(2,1)S(1)} fusion(bf16[4,256,512]{1,2,0:T(8,128)(2,1)S(1)} %copy-done.3, f32[4,256,512]{1,2,0:T(8,128)S(1)} %get-tuple-element.34, f32[4,512]{1,0:T(4,128)S(1)} %get-tuple-element.35, f32[4,512]{1,0:T(4,128)S(1)} %get-tuple-element.28, f32[4,512]{1,0:T(4,128)S(1)} %get-tuple-element.36, ...), kind=kLoop, calls=%fused_computation.9 | loop fusion | flops 4718592 | bytes 4235264 | tf_op jit(solution)/shard_map/convert_element_type | solution.py:71
  51.1 0.6 fusion.25
  51.7 0.5 fusion.24
  52.2 0.6 fusion.23
  52.8 0.6 fusion.22
  53.4 0.5 fusion.21
  53.9 0.6 fusion.20
  54.4 0.6 fusion.19
  55.0 0.5 fusion.18
  55.5 0.6 fusion.17
  56.1 1.4 copy-done.6
  57.7 1.3 collective-permute-start.2
  59.0 3.2 %collective-permute-start.3 = (bf16[1,256,512]{1,2,0:T(8,128)(2,1)S(1)}, bf16[1,256,512]{1,2,0:T(8,128)(2,1)S(1)}, u32[]{:S(2)}, u32[]{:S(2)}) collective-permute-start(bf16[1,256,512]{1,2,0:T(8,128)(2,1)S(1)} %get-tuple-element.23), channel_id=1, source_target_pairs={{0,4},{4,8},{8,12},{12,16},{16,20},{20,24},{24,28},{1,5},{5,9},{9,... | collective-permute-start | bytes 786440 | tf_op jit(solution)/shard_map/ppermute | solution.py:14
  62.2 2.8 %fusion.33 = f32[4,512,256]{2,1,0:T(8,128)} fusion(pred[512]{0:T(512)(128)(4,1)S(1)} %compare_and_fusion, bf16[4,256,512]{1,2,0:T(8,128)(2,1)S(1)} %multiply_convert_fusion, bf16[3,3,256,256]{3,2,1,0:T(8,128)(2,1)} %all-gather.2.cloned.1.call-done), kind=kOutput, calls=%fused_computation.62 | convolution fusion | flops 268959744 | bytes 3277312 | tf_op jit(solution)/shard_map/hok,oi->hik/dot_general | solution.py:89
  65.0 2.7 %fusion.59 = f32[4,512,256]{2,1,0:T(8,128)} fusion(bf16[4,256,512]{1,2,0:T(8,128)(2,1)S(1)} %multiply_convert_fusion, bf16[3,3,256,256]{3,2,1,0:T(8,128)(2,1)} %all-gather.2.cloned.1.call-done), kind=kOutput, calls=%fused_computation.103 | convolution fusion | flops 268435456 | bytes 3276800 | tf_op jit(solution)/shard_map/hok,oi->hik/dot_general | solution.py:89
  67.7 2.7 %fusion.36 = f32[4,512,256]{2,1,0:T(8,128)} fusion(pred[512]{0:T(512)(128)(4,1)S(1)} %compare_and_fusion.1, bf16[4,256,512]{1,2,0:T(8,128)(2,1)S(1)} %multiply_convert_fusion, bf16[3,3,256,256]{3,2,1,0:T(8,128)(2,1)} %all-gather.2.cloned.1.call-done), kind=kOutput, calls=%fused_computation.65 | convolution fusion | flops 268959744 | bytes 3277312 | tf_op jit(solution)/shard_map/hok,oi->hik/dot_general | solution.py:89
  70.9 1.0 copy-done.5
  72.3 1.8 %fusion.31 = f32[4,512,256]{2,1,0:T(8,128)} fusion(bf16[4,256,514]{1,2,0:T(8,128)(2,1)S(1)} %get-tuple-element.20, pred[512]{0:T(512)(128)(4,1)S(1)} %compare_and_fusion, bf16[3,3,256,256]{3,2,1,0:T(8,128)(2,1)S(1)} %copy-done.5), kind=kOutput, calls=%fused_computation.57 | convolution fusion | flops 268959744 | bytes 3277312 | tf_op jit(solution)/shard_map/hok,oi->hik/dot_general | solution.py:89
  74.1 1.9 %fusion.32 = f32[4,512,256]{2,1,0:T(8,128)} fusion(bf16[4,256,514]{1,2,0:T(8,128)(2,1)S(1)} %get-tuple-element.20, pred[512]{0:T(512)(128)(4,1)S(1)} %compare_and_fusion.1, bf16[3,3,256,256]{3,2,1,0:T(8,128)(2,1)S(1)} %copy-done.5), kind=kOutput, calls=%fused_computation.59 | convolution fusion | flops 268959744 | bytes 3277312 | tf_op jit(solution)/shard_map/hok,oi->hik/dot_general | solution.py:89
  75.9 1.9 %fusion.30 = f32[4,512,256]{2,1,0:T(8,128)} fusion(bf16[4,256,514]{1,2,0:T(8,128)(2,1)S(1)} %get-tuple-element.21, pred[512]{0:T(512)(128)(4,1)S(1)} %compare_and_fusion.1, bf16[3,3,256,256]{3,2,1,0:T(8,128)(2,1)S(1)} %copy-done.5), kind=kOutput, calls=%fused_computation.55 | convolution fusion | flops 268959744 | bytes 3277312 | tf_op jit(solution)/shard_map/hok,oi->hik/dot_general | solution.py:89
  77.8 1.8 %fusion.29 = f32[4,512,256]{2,1,0:T(8,128)} fusion(bf16[4,256,514]{1,2,0:T(8,128)(2,1)S(1)} %get-tuple-element.21, pred[512]{0:T(512)(128)(4,1)S(1)} %compare_and_fusion, bf16[3,3,256,256]{3,2,1,0:T(8,128)(2,1)S(1)} %copy-done.5), kind=kOutput, calls=%fused_computation.53 | convolution fusion | flops 268959744 | bytes 3277312 | tf_op jit(solution)/shard_map/hok,oi->hik/dot_general | solution.py:89
  79.6 15.5 %reduce-scatter.2.cloned.1.call-done = f32[3,3,64,256]{3,2,1,0:T(8,128)} async-done(((f32[3,3,256,256]{3,2,1,0:T(8,128)}), f32[3,3,64,256]{3,2,1,0:T(8,128)}) %reduce-scatter.2.cloned.1.call-update) | async-done | bytes 589840 | tf_op jit(solution)/shard_map/reduce_scatter | solution.py:80
  95.1 7.2 %fusion.2 = bf16[4,256,512]{1,2,0:T(8,128)(2,1)} fusion(f32[4,512,256]{2,1,0:T(8,128)} %fusion.29, f32[4,512,256]{2,1,0:T(8,128)} %fusion.30, f32[4,512,256]{2,1,0:T(8,128)} %fusion.33, f32[4,512,256]{2,1,0:T(8,128)} %fusion.59, f32[4,512,256]{2,1,0:T(8,128)} %fusion.36, f32[4,512,256]{2,1,0:T(8,128)} %fusion.31, f32[4,512,256]{2,1,0:T(8,128)} %fusion.32, ...), kind=kOutput, calls=%fused_computation.15 | convolution fusion | flops 275775488 | bytes 19267584 | tf_op jit(solution)/shard_map/hok,oi->hik/dot_general | solution.py:89
  102.4 2.3 %copy.30 = bf16[4,256,512]{2,1,0:T(8,128)(2,1)} copy(bf16[4,256,512]{1,2,0:T(8,128)(2,1)} %fusion.2) | data formatting | bytes 2097152
  104.6 49.8 %all-reduce.8.cloned.1.call-done = f32[3,3,64,256]{3,2,1,0:T(8,128)} async-done(((f32[3,3,64,256]{3,2,1,0:T(8,128)}), f32[3,3,64,256]{3,2,1,0:T(8,128)}) %all-reduce.8.cloned.1.call-update) | async-done | bytes 589840 | tf_op jit(solution)/shard_map/psum | solution.py:81
  154.4 1.9 %copy.58 = f32[3,3,64,256]{3,2,1,0:T(8,128)} copy(f32[3,3,64,256]{3,2,1,0:T(8,128)} %all-reduce.8.cloned.1.call-done) | data formatting | bytes 1179648
  (40 shorter events, 1.3 us)
Async XLA Ops:
  7.2 6.1 %copy-start.10 = (s32[16]{0:T(128)S(1)}, s32[16]{0:T(128)}, u32[]{:S(2)}) copy-start(s32[16]{0:T(128)} %param.9) | copy-start | bytes 196
  7.2 9.4 %copy-start.9 = (bf16[4,256,512]{2,1,0:T(8,128)(2,1)S(1)}, bf16[4,256,512]{2,1,0:T(8,128)(2,1)}, u32[]{:S(2)}) copy-start(bf16[4,256,512]{2,1,0:T(8,128)(2,1)} %param.8) | copy-start | bytes 3145732
  7.2 33.0 %all-gather.2.cloned.1.call-start = ((), (), s32[]{:S(2)}) async-start(), calls=%async_computation.1 | async-start | bytes 1474560 | tf_op jit(solution)/shard_map/all_gather | solution.py:40
  7.9 87.2 %reduce-scatter.2.cloned.1.call-start = ((), (), s32[]{:S(2)}) async-start(), calls=%async_computation.2 | async-start | bytes 2949120 | tf_op jit(solution)/shard_map/reduce_scatter | solution.py:80
  9.5 8.5 %collective-permute-start = (bf16[1,256,512]{1,2,0:T(8,128)(2,1)S(1)}, bf16[1,256,512]{1,2,0:T(8,128)(2,1)S(1)}, u32[]{:S(2)}, u32[]{:S(2)}) collective-permute-start(bf16[1,256,512]{1,2,0:T(8,128)(2,1)S(1)} %get-tuple-element.26), channel_id=1, source_target_pairs={{0,4},{4,8},{8,12},{12,16},{16,20},{20,24},{24,28},{1,5},{5,9},{9,... | collective-permute-start | bytes 786440 | tf_op jit(solution)/shard_map/ppermute | solution.py:14
  11.9 6.8 %collective-permute-start.1 = (bf16[1,256,512]{1,2,0:T(8,128)(2,1)S(1)}, bf16[1,256,512]{1,2,0:T(8,128)(2,1)S(1)}, u32[]{:S(2)}, u32[]{:S(2)}) collective-permute-start(bf16[1,256,512]{1,2,0:T(8,128)(2,1)S(1)} %get-tuple-element.27), channel_id=1, source_target_pairs={{4,0},{8,4},{12,8},{16,12},{20,16},{24,20},{28,24},{5,1},{9,5},{13... | collective-permute-start | bytes 786440 | tf_op jit(solution)/shard_map/ppermute | solution.py:17
  18.0 0.7 copy-start.7
  19.8 22.3 %copy-start = (bf16[4,256,512]{1,2,0:T(8,128)(2,1)}, bf16[4,256,512]{1,2,0:T(8,128)(2,1)S(1)}, u32[]{:S(2)}) copy-start(bf16[4,256,512]{1,2,0:T(8,128)(2,1)S(1)} %get-tuple-element.24) | copy-start | bytes 3145732
  40.2 1.5 copy-start.4
  42.7 1.0 copy-start.8
  44.6 1.2 copy-start.2
  46.4 1.4 copy-start.3
  49.4 1.7 %copy-start.1 = (bf16[4,256,512]{1,2,0:T(8,128)(2,1)S(1)}, bf16[4,256,512]{1,2,0:T(8,128)(2,1)}, u32[]{:S(2)}) copy-start(bf16[4,256,512]{1,2,0:T(8,128)(2,1)} %copy-done) | copy-start | bytes 3145732
  56.1 1.4 copy-start.6
  57.6 96.9 %all-reduce.8.cloned.1.call-start = ((), (), s32[]{:S(2)}) async-start(), calls=%async_computation.3 | async-start | bytes 1179648 | tf_op jit(solution)/shard_map/psum | solution.py:81
  57.7 12.8 %collective-permute-start.2 = (bf16[1,256,512]{1,2,0:T(8,128)(2,1)S(1)}, bf16[1,256,512]{1,2,0:T(8,128)(2,1)S(1)}, u32[]{:S(2)}, u32[]{:S(2)}) collective-permute-start(bf16[1,256,512]{1,2,0:T(8,128)(2,1)S(1)} %get-tuple-element.22), channel_id=1, source_target_pairs={{4,0},{8,4},{12,8},{16,12},{20,16},{24,20},{28,24},{5,1},{9,5},{13... | collective-permute-start | bytes 786440 | tf_op jit(solution)/shard_map/ppermute | solution.py:17
  59.0 11.5 %collective-permute-start.3 = (bf16[1,256,512]{1,2,0:T(8,128)(2,1)S(1)}, bf16[1,256,512]{1,2,0:T(8,128)(2,1)S(1)}, u32[]{:S(2)}, u32[]{:S(2)}) collective-permute-start(bf16[1,256,512]{1,2,0:T(8,128)(2,1)S(1)} %get-tuple-element.23), channel_id=1, source_target_pairs={{0,4},{4,8},{8,12},{12,16},{16,20},{20,24},{24,28},{1,5},{5,9},{9,... | collective-permute-start | bytes 786440 | tf_op jit(solution)/shard_map/ppermute | solution.py:14
  70.5 1.4 copy-start.5
Sparse Core Ops, SparseCore 0:
  9.8 30.2 all-gather.1
  57.7 37.3 reduce-scatter.1
  97.5 56.9 all-reduce.7
where the time goes:
time: 163 us
  waiting for transfers between devices  86.4 us (53%)
  matrix products  34.5 us (21%)
  between operations  14.1 us (9%)
  local copies, waits for them, and re-layouts  12.1 us (7%)
  starting transfers between devices  8.34 us (5%)
  other arithmetic  7.45 us (5%)
    psum x1, waiting for transfers between devices, body(): weight_grad = lax.psum(share, 'rows')  49.8 us
    dot_general x9, matrix products, body(): jnp.einsum('hok,oi->hik', window, kernel[offset_row, offset_col], preferr...  23.2 us
    all_gather x1, waiting for transfers between devices, body(): kernel = lax.all_gather(conv_weight, 'ch', axis=2, tiled=True)  20.3 us
    reduce_scatter x1, waiting for transfers between devices, body(): share = lax.psum_scatter(weight_part, 'ch', scatter_dimension=2, tiled=True)  15.5 us
    unnamed x26, local copies, waits for them, and re-layouts  11.3 us
    dot_general x9, matrix products, body(): jnp.einsum('hik,oi->hok', window, kernel[offset_row, offset_col], preferr...  6.34 us
    ppermute x2, starting transfers between devices, padded_2(): lax.ppermute(lax.slice_in_dim(block, block.shape[dim] - width, None, axis...  5.64 us
    dot_general x9, matrix products, body(): jnp.einsum('hik,hok->oi', window, grad_pre, preferred_element_type=jnp.fl...  4.98 us
  transfers between devices with their start and end apart: 7, of which 3 were waited for; matrix products, arithmetic and copies ran while one was open for 20% of the time, Pallas kernels for 0%

commit v1 on v0

v1 whole, which is shorter than its diff:
```python
import functools

import jax
import jax.numpy as jnp
from jax import lax
from jax.experimental import pallas as pl
from jax.experimental.pallas import tpu as pltpu
from jax.sharding import PartitionSpec as P

COLS = 128
LANES = 128
F32 = jnp.float32
BF16 = jnp.bfloat16


def kernel(
    rows_n, ch_n, split_z,
    feat, weight, cot, valid,
    in_grad, w_grad,
    xs, gs, wf, wt, cv, ig, own, sib_s, sib_r, ch_s, ch_r, z_s, z_r, fin, wout,
    loc, out_sem, xh_s, xh_r, gh_s, gh_r, ws, wr, fs, fr,
    sb_s, sb_r, cs, cr, zs_s, zs_r, ag_s, ag_r, fn_s, fn_r,
):
    band, total, cells = feat.shape
    imgs = cells // COLS
    part = weight.shape[1]
    zn = rows_n // 2
    piece = part // zn if split_z else part
    row = lax.axis_index("rows")
    chn = lax.axis_index("ch")
    core = lax.rem(row, 2)
    z = row // 2
    sib = row + 1 - 2 * core

    def ch_at(d):
        return lax.rem(chn + d, ch_n)

    def ch_from(d):
        return lax.rem(chn + ch_n - d, ch_n)

    def z_at(d):
        return lax.rem(z + d, zn)

    def z_from(d):
        return lax.rem(z + zn - d, zn)

    def remote(src, dst, send, recv, r, c):
        return pltpu.make_async_remote_copy(
            src_ref=src, dst_ref=dst, send_sem=send, recv_sem=recv,
            device_id=(r, c), device_id_type=pl.DeviceIdType.MESH,
        )

    has_up = row > 0
    has_dn = row < rows_n - 1

    l_feat = pltpu.make_async_copy(feat, xs.at[1:band + 1, total:2 * total, :], loc.at[0])
    l_cot = pltpu.make_async_copy(cot, cv, loc.at[1])
    l_w = pltpu.make_async_copy(
        weight, wf.at[:, pl.ds(pl.multiple_of(chn * part, part), part), :], loc.at[2]
    )
    l_feat.start()
    l_w.start()
    l_cot.start()

    barrier = pltpu.get_barrier_semaphore()
    for d in range(1, rows_n):
        pl.semaphore_signal(
            barrier, inc=1, device_id=(lax.rem(row + d, rows_n), chn),
            device_id_type=pl.DeviceIdType.MESH,
        )
    for d in range(1, ch_n):
        pl.semaphore_signal(
            barrier, inc=1, device_id=(row, ch_at(d)), device_id_type=pl.DeviceIdType.MESH
        )
    pl.semaphore_wait(barrier, rows_n - 1 + ch_n - 1)

    half = pl.ds(pl.multiple_of(core * LANES, LANES), LANES)
    other_half = pl.ds(pl.multiple_of((1 - core) * LANES, LANES), LANES)

    def o_slice(c):
        return pl.ds(pl.multiple_of(c * part, part), part)

    w_sends = [
        remote(weight.at[:, :, half], wf.at[:, o_slice(chn), half],
               ws.at[d - 1], wr.at[d - 1], row, ch_at(d))
        for d in range(1, ch_n)
    ]
    w_recvs = [
        remote(weight.at[:, :, half], wf.at[:, o_slice(ch_from(d)), half],
               ws.at[d - 1], wr.at[d - 1], row, ch_at(d))
        for d in range(1, ch_n)
    ]
    for copy in w_sends:
        copy.start()

    def halo(buf, source_top, source_bottom, send, recv):
        up = remote(source_top, buf.at[band + 1, total:2 * total, :],
                    send.at[0], recv.at[0], row - 1, chn)
        dn = remote(source_bottom, buf.at[0, total:2 * total, :],
                    send.at[1], recv.at[1], row + 1, chn)
        return up, dn

    x_up, x_dn = halo(xs, feat.at[0], feat.at[band - 1], xh_s, xh_r)

    def halo_start(up, dn):
        @pl.when(has_up)
        def _():
            up.start()

        @pl.when(has_dn)
        def _():
            dn.start()

    def halo_finish(buf, up, dn):
        @pl.when(has_up)
        def _():
            up.wait_send()
            dn.wait_recv()

        @pl.when(has_dn)
        def _():
            dn.wait_send()
            up.wait_recv()

        @pl.when(jnp.logical_not(has_up))
        def _():
            buf[0, total:2 * total, :] = jnp.zeros((total, cells), BF16)

        @pl.when(jnp.logical_not(has_dn))
        def _():
            buf[band + 1, total:2 * total, :] = jnp.zeros((total, cells), BF16)

    halo_start(x_up, x_dn)

    lane = lax.broadcasted_iota(jnp.int32, (total, COLS), 1)
    before, after = 0, 2 * total

    def shift_row(buf, p, minus_at, plus_at):
        for n in range(imgs):
            cols = pl.ds(n * COLS, COLS)
            v = buf[p, total:2 * total, cols].astype(F32)
            minus = jnp.where(lane == 0, 0.0, pltpu.roll(v, 1, 1))
            plus = jnp.where(lane == COLS - 1, 0.0, pltpu.roll(v, COLS - 1, 1))
            buf[p, minus_at:minus_at + total, cols] = minus.astype(BF16)
            buf[p, plus_at:plus_at + total, cols] = plus.astype(BF16)

    l_feat.wait()

    def shift_x(s, carry):
        shift_row(xs, s + 1, before, after)
        return carry

    lax.fori_loop(0, band, shift_x, 0)
    halo_finish(xs, x_up, x_dn)

    def shift_x_edge(s, carry):
        shift_row(xs, s * (band + 1), before, after)
        return carry

    lax.fori_loop(0, 2, shift_x_edge, 0)

    f_sends, f_recvs = [], []
    for d in range(1, ch_n):
        w_recvs[d - 1].wait_recv()
        here = wf.at[:, o_slice(ch_from(d)), half]
        there = wf.at[:, o_slice(ch_from(d)), other_half]
        send = remote(here, here, fs.at[d - 1], fr.at[d - 1], sib, chn)
        send.start()
        f_sends.append(send)
        f_recvs.append(remote(there, there, fs.at[d - 1], fr.at[d - 1], sib, chn))
    l_w.wait()
    l_cot.wait()
    for copy in f_recvs:
        copy.wait_recv()

    def forward(h):
        w_all = jnp.concatenate([wf[t] for t in range(9)], axis=1)
        x_all = jnp.concatenate([xs[h], xs[h + 1], xs[h + 2]], axis=0)
        summed = jnp.dot(w_all, x_all, preferred_element_type=F32)
        center = jnp.sum(summed, 0, keepdims=True) / total
        spread = jnp.sum(summed * summed, 0, keepdims=True) / total - center * center
        inverse = lax.rsqrt(spread + 1e-06)
        normed = (summed - center) * inverse
        keep = jnp.concatenate(
            [
                jnp.full((1, COLS), (row * band + h < valid[chn * imgs + n]).astype(F32))
                for n in range(imgs)
            ],
            axis=1,
        )
        masked = cv[h].astype(F32) * keep
        mean = jnp.sum(masked, 0, keepdims=True) / total
        cross = jnp.sum(masked * normed, 0, keepdims=True) / total
        gs[h + 1, total:2 * total, :] = (inverse * (masked - mean - normed * cross)).astype(BF16)

    def edge_row(s, carry):
        forward(s * (band - 1))
        return carry

    lax.fori_loop(0, 2, edge_row, 0)
    g_up, g_dn = halo(
        gs, gs.at[1, total:2 * total, :], gs.at[band, total:2 * total, :], gh_s, gh_r
    )
    halo_start(g_up, g_dn)

    def mid_row(s, carry):
        forward(s + 1)
        return carry

    lax.fori_loop(0, band - 2, mid_row, 0)

    sib_copies = []

    def weight_step(r):
        grads = jnp.concatenate([gs[h + 1, total:2 * total, :] for h in range(band)], axis=1)
        for c in range(3):
            window = jnp.concatenate(
                [xs[h + r, c * total:(c + 1) * total, :] for h in range(band)], axis=1
            )
            term = lax.dot_general(
                grads, window, (((1,), (1,)), ((), ())), preferred_element_type=F32
            )
            low, high = term[:, :LANES], term[:, LANES:]
            own[3 * r + c] = jnp.where(core == 0, low, high)
            sib_s[3 * r + c] = jnp.where(core == 0, high, low).astype(BF16)
        group = pl.ds(3 * r, 3)
        copy = remote(sib_s.at[group], sib_r.at[group], sb_s.at[r], sb_r.at[r], sib, chn)
        copy.start()
        sib_copies.append(copy)

    ch_sends = []

    def combine(g):
        sib_copies[g].wait_recv()
        for t in range(3 * g, 3 * g + 3):
            both = own[t] + sib_r[t].astype(F32)
            own[t] = both
            ch_s[t] = both.astype(BF16)
        group = pl.ds(3 * g, 3)
        for d in range(1, ch_n):
            copy = remote(
                ch_s.at[group, o_slice(ch_at(d)), :], ch_r.at[d - 1, group],
                cs.at[g, d - 1], cr.at[g, d - 1], row, ch_at(d),
            )
            copy.start()
            ch_sends.append(copy)

    z_sends = []

    def z_piece(j):
        return pl.ds(pl.multiple_of(j * piece, piece), piece) if split_z else pl.ds(0, piece)

    def plane_sum(g):
        group = pl.ds(3 * g, 3)
        for d in range(1, ch_n):
            ch_sends[g * (ch_n - 1) + d - 1].wait_recv()
        acc = own[group, o_slice(chn), :]
        for d in range(1, ch_n):
            acc = acc + ch_r[d - 1, group].astype(F32)
        z_s[group] = acc.astype(BF16)
        for d in range(1, zn):
            copy = remote(
                z_s.at[group, z_piece(z_at(d)), :], z_r.at[z, group],
                zs_s.at[g, d - 1], zs_r.at[g, d - 1], 2 * z_at(d) + core, chn,
            )
            copy.start()
            z_sends.append(copy)

    ag_sends = []

    def line_sum(g):
        group = pl.ds(3 * g, 3)
        z_r[z, group] = z_s[group, z_piece(z), :]
        for d in range(1, zn):
            src = z_s.at[group, z_piece(z_at(d)), :]
            remote(src, z_r.at[z_from(d), group], zs_s.at[g, d - 1], zs_r.at[g, d - 1],
                   2 * z_at(d) + core, chn).wait_recv()
        acc = z_r[0, group].astype(F32)
        for s in range(1, zn):
            acc = acc + z_r[s, group].astype(F32)
        fin[core, group, z_piece(z), :] = acc.astype(BF16)
        if split_z:
            mine = fin.at[core, group, z_piece(z), :]
            for d in range(1, zn):
                copy = remote(mine, mine, ag_s.at[g, d - 1], ag_r.at[g, d - 1],
                              2 * z_at(d) + core, chn)
                copy.start()
                ag_sends.append(copy)

    fin_sends = []

    def pass_on(g):
        group = pl.ds(3 * g, 3)
        if split_z:
            for d in range(1, zn):
                theirs = fin.at[core, group, z_piece(z_from(d)), :]
                remote(theirs, theirs, ag_s.at[g, d - 1], ag_r.at[g, d - 1],
                       2 * z_at(d) + core, chn).wait_recv()
        copy = remote(fin.at[core, group], fin.at[core, group],
                      fn_s.at[g], fn_r.at[g], sib, chn)
        copy.start()
        fin_sends.append(copy)

    def transpose_taps(t, carry):
        r, c = t // 3, lax.rem(t, 3)
        at = pl.multiple_of(((2 - r) * 3 + c) * total, total)
        wt[:, pl.ds(at, total)] = wf[t].T
        return carry

    def shift_g(s, carry):
        shift_row(gs, s + 1, after, before)
        return carry

    def shift_g_edge(s, carry):
        shift_row(gs, s * (band + 1), after, before)
        return carry

    out_copies = []

    def input_row(h):
        g_all = jnp.concatenate([gs[h], gs[h + 1], gs[h + 2]], axis=0)
        ig[h] = jnp.dot(wt[...], g_all, preferred_element_type=F32).astype(BF16)

    def input_out(h):
        copy = pltpu.make_async_copy(ig.at[h], in_grad.at[h], out_sem.at[h])
        copy.start()
        out_copies.append(copy)

    def input_edges(s, carry):
        input_row(s * (band - 1))
        return carry

    def input_mid(s, carry):
        input_row(s + 1)
        return carry

    weight_step(0)
    weight_step(1)
    combine(0)
    weight_step(2)
    combine(1)
    lax.fori_loop(0, 9, transpose_taps, 0)
    combine(2)
    plane_sum(0)
    lax.fori_loop(0, band, shift_g, 0)
    plane_sum(1)
    halo_finish(gs, g_up, g_dn)
    lax.fori_loop(0, 2, shift_g_edge, 0)
    plane_sum(2)
    line_sum(0)
    lax.fori_loop(0, band - 2, input_mid, 0)
    for h in range(1, band - 1):
        input_out(h)
    line_sum(1)
    line_sum(2)
    pass_on(0)
    lax.fori_loop(0, 2, input_edges, 0)
    for h in (0, band - 1):
        input_out(h)
    pass_on(1)
    pass_on(2)
    w_outs = []
    for g in range(3):
        group = pl.ds(3 * g, 3)
        remote(fin.at[core, group], fin.at[1 - core, group],
               fn_s.at[g], fn_r.at[g], sib, chn).wait_recv()
        wout[group, :, :LANES] = fin[0, group].astype(F32)
        wout[group, :, LANES:] = fin[1, group].astype(F32)
        copy = pltpu.make_async_copy(wout.at[group], w_grad.at[group], out_sem.at[band + g])
        copy.start()
        w_outs.append(copy)

    for copy in w_sends + f_sends + sib_copies + ch_sends + z_sends + ag_sends + fin_sends:
        copy.wait_send()
    for copy in out_copies + w_outs:
        copy.wait()


def body(rows_n, ch_n, features, conv_weight, cotangent, valid_rows):
    band, total, cells = features.shape
    part = conv_weight.shape[2]
    zn = rows_n // 2
    split_z = part % (16 * zn) == 0
    piece = part // zn if split_z else part
    dma = pltpu.SemaphoreType.DMA
    anywhere = pl.BlockSpec(memory_space=pl.ANY)
    in_grad, w_grad = pl.pallas_call(
        functools.partial(kernel, rows_n, ch_n, split_z),
        out_shape=(
            jax.ShapeDtypeStruct((band, total, cells), BF16),
            jax.ShapeDtypeStruct((9, part, total), F32),
        ),
        in_specs=[anywhere, anywhere, anywhere, pl.BlockSpec(memory_space=pltpu.SMEM)],
        out_specs=(anywhere, anywhere),
        scratch_shapes=[
            pltpu.VMEM((band + 2, 3 * total, cells), BF16),
            pltpu.VMEM((band + 2, 3 * total, cells), BF16),
            pltpu.VMEM((9, total, total), BF16),
            pltpu.VMEM((total, 9 * total), BF16),
            pltpu.VMEM((band, total, cells), BF16),
            pltpu.VMEM((band, total, cells), BF16),
            pltpu.VMEM((9, total, LANES), F32),
            pltpu.VMEM((9, total, LANES), BF16),
            pltpu.VMEM((9, total, LANES), BF16),
            pltpu.VMEM((9, total, LANES), BF16),
            pltpu.VMEM((ch_n - 1, 9, part, LANES), BF16),
            pltpu.VMEM((9, part, LANES), BF16),
            pltpu.VMEM((zn, 9, piece, LANES), BF16),
            pltpu.VMEM((2, 9, part, LANES), BF16),
            pltpu.VMEM((9, part, total), F32),
            dma((3,)), dma((band + 3,)),
            dma((2,)), dma((2,)), dma((2,)), dma((2,)),
            dma((ch_n - 1,)), dma((ch_n - 1,)), dma((ch_n - 1,)), dma((ch_n - 1,)),
            dma((3,)), dma((3,)),
            dma((3, ch_n - 1)), dma((3, ch_n - 1)),
            dma((3, zn - 1)), dma((3, zn - 1)),
            dma((3, zn - 1)), dma((3, zn - 1)),
            dma((3,)), dma((3,)),
        ],
        compiler_params=pltpu.CompilerParams(
            collective_id=0, has_side_effects=True, vmem_limit_bytes=56 * 1024 * 1024
        ),
        name="pyramid_backward",
    )(features, conv_weight.reshape(9, part, total), cotangent, valid_rows)
    return in_grad, w_grad.reshape(3, 3, part, total)


def solution(mesh):
    in_specs = (P("rows", None, "ch"), P(None, None, "ch", None), P("rows", None, "ch"), P())
    out_specs = (P("rows", None, "ch"), P(None, None, "ch", None))
    step = functools.partial(body, mesh.shape["rows"], mesh.shape["ch"])
    return jax.shard_map(step, mesh=mesh, in_specs=in_specs, out_specs=out_specs, check_vma=False)
```

time: 163 us -> 45.4 us (0.28)
  waiting for transfers between devices: 86.4 us -> 0 us
  Pallas kernels: 0 us -> 40.9 us
  matrix products: 34.5 us -> 0 us
  between operations: 14.1 us -> 0.65 us
  local copies, waits for them, and re-layouts: 12.1 us -> 3.14 us
  starting transfers between devices: 8.34 us -> 0 us
  other arithmetic: 7.45 us -> 0 us
    psum x1 -> x0, waiting for transfers between devices: 49.8 us -> none  [body(): weight_grad = lax.psum(share, 'rows')]
    pallas_call x0 -> x1, Pallas kernels: none -> 40.9 us  [body(): pl.pallas_call(functools.partial(kernel, rows_n, ch_n, split_z), out_shap...]
    dot_general x27 -> x0, matrix products: 34.5 us -> none  [the longest x9 23.2 us: body(): jnp.einsum('hok,oi->hik', window, kernel[offset_row, offset_col], preferr...]
    all_gather x1 -> x0, waiting for transfers between devices: 20.3 us -> none  [body(): kernel = lax.all_gather(conv_weight, 'ch', axis=2, tiled=True)]
    reduce_scatter x1 -> x0, waiting for transfers between devices: 15.5 us -> none  [body(): share = lax.psum_scatter(weight_part, 'ch', scatter_dimension=2, tiled=True)]
    ppermute x4 -> x0, starting transfers between devices: 8.22 us -> none  [the longest x2 5.64 us: padded_2(): lax.ppermute(lax.slice_in_dim(block, block.shape[dim] - width, None, axis...]
    unnamed x26 -> x4, local copies, waits for them, and re-layouts: 11.3 us -> 3.14 us
    gather x1 -> x0, other arithmetic: 2.55 us -> none  [body(): limits = jnp.repeat(local_limits, columns, total_repeat_length=cells)]
  transfers between devices with their start and end apart: 7 -> 0, of which waited for: 3 -> 0; matrix products, arithmetic and copies ran while one was open for 20% -> 0% of each run, Pallas kernels for 0% -> 0%
where the time goes in v1:
time: 45.4 us; the launch traced here: 44.7 us
  Pallas kernels  40.9 us (90%)
  local copies, waits for them, and re-layouts  3.14 us (7%)
  between operations  0.65 us (1%)
    pallas_call x1, Pallas kernels, body(): pl.pallas_call(functools.partial(kernel, rows_n, ch_n, split_z), out_shap...  40.9 us
    unnamed x4, local copies, waits for them, and re-layouts  3.14 us

profile of v1, /device:TPU:0, one launch (start us, length us, event | category | flops | bytes accessed | tf_op | source)
XLA Modules:
  0.0 44.7 jit_solution(5866367469515498518)
XLA Ops:
  0.6 40.9 %pyramid_backward.1 = (bf16[4,256,512]{2,1,0:T(8,128)(2,1)}, f32[9,64,256]{2,1,0:T(8,128)}) custom-call(bf16[4,256,512]{2,1,0:T(8,128)(2,1)} %feat.1, bf16[9,64,256]{2,1,0:T(8,128)(2,1)} %bitcast.3, bf16[4,256,512]{2,1,0:T(8,128)(2,1)} %cot.1, s32[16]{0:T(128)} %valid.1), custom_call_target="tpu_custom_call" | custom-call | tf_op jit(solution)/shard_map/pyramid_backward/pallas_call | solution.py:387
  41.5 0.0 copy-start
  41.5 2.3 %copy.8 = bf16[4,256,512]{2,1,0:T(8,128)(2,1)} copy(bf16[4,256,512]{2,1,0:T(8,128)(2,1)} %get-tuple-element.8) | data formatting | bytes 2097152
  43.9 0.0 copy-done
  43.9 0.8 %copy.9 = f32[3,3,64,256]{3,2,1,0:T(8,128)} copy(f32[3,3,64,256]{3,2,1,0:T(8,128)S(1)} %bitcast.2) | data formatting | bytes 1179648
Async XLA Ops:
  41.5 2.3 %copy-start = (f32[9,64,256]{2,1,0:T(8,128)S(1)}, f32[9,64,256]{2,1,0:T(8,128)}, u32[]{:S(2)}) copy-start(f32[9,64,256]{2,1,0:T(8,128)} %get-tuple-element.5) | copy-start | bytes 1769476

commit v2 on v1

--- a/solution.py
+++ b/solution.py
@@ -11,14 +11,15 @@
 LANES = 128
 F32 = jnp.float32
 BF16 = jnp.bfloat16
+GROUPS = [(0, 2), (2, 2), (4, 2), (6, 2), (8, 1)]
 
 
 def kernel(
     rows_n, ch_n, split_z,
     feat, weight, cot, valid,
     in_grad, w_grad,
-    xs, gs, wf, wt, cv, ig, own, sib_s, sib_r, ch_s, ch_r, z_s, z_r, fin, wout,
-    loc, out_sem, xh_s, xh_r, gh_s, gh_r, ws, wr, fs, fr,
+    xs, gs, wf, wt, cv, own, sib_s, sib_r, ch_s, ch_r, z_s, z_r, fin,
+    loc, xh_s, xh_r, gh_s, gh_r, ws, wr, fs, fr,
     sb_s, sb_r, cs, cr, zs_s, zs_r, ag_s, ag_r, fn_s, fn_r,
 ):
     band, total, cells = feat.shape
@@ -209,11 +210,15 @@
 
     lax.fori_loop(0, band - 2, mid_row, 0)
 
-    sib_copies = []
-
-    def weight_step(r):
-        grads = jnp.concatenate([gs[h + 1, total:2 * total, :] for h in range(band)], axis=1)
-        for c in range(3):
+    sib_copies = {}
+
+    def weight_step(g):
+        first, count = GROUPS[g]
+        for t in range(first, first + count):
+            r, c = divmod(t, 3)
+            grads = jnp.concatenate(
+                [gs[h + 1, total:2 * total, :] for h in range(band)], axis=1
+            )
             window = jnp.concatenate(
                 [xs[h + r, c * total:(c + 1) * total, :] for h in range(band)], axis=1
             )
@@ -221,39 +226,40 @@
                 grads, window, (((1,), (1,)), ((), ())), preferred_element_type=F32
             )
             low, high = term[:, :LANES], term[:, LANES:]
-            own[3 * r + c] = jnp.where(core == 0, low, high)
-            sib_s[3 * r + c] = jnp.where(core == 0, high, low).astype(BF16)
-        group = pl.ds(3 * r, 3)
-        copy = remote(sib_s.at[group], sib_r.at[group], sb_s.at[r], sb_r.at[r], sib, chn)
+            own[t] = jnp.where(core == 0, low, high)
+            sib_s[t] = jnp.where(core == 0, high, low).astype(BF16)
+        group = pl.ds(first, count)
+        copy = remote(sib_s.at[group], sib_r.at[group], sb_s.at[g], sb_r.at[g], sib, chn)
         copy.start()
-        sib_copies.append(copy)
-
-    ch_sends = []
+        sib_copies[g] = copy
+
+    sends = []
+    ch_copies = {}
 
     def combine(g):
+        first, count = GROUPS[g]
         sib_copies[g].wait_recv()
-        for t in range(3 * g, 3 * g + 3):
+        for t in range(first, first + count):
             both = own[t] + sib_r[t].astype(F32)
             own[t] = both
             ch_s[t] = both.astype(BF16)
-        group = pl.ds(3 * g, 3)
+        group = pl.ds(first, count)
         for d in range(1, ch_n):
             copy = remote(
                 ch_s.at[group, o_slice(ch_at(d)), :], ch_r.at[d - 1, group],
                 cs.at[g, d - 1], cr.at[g, d - 1], row, ch_at(d),
             )
             copy.start()
-            ch_sends.append(copy)
-
-    z_sends = []
+            sends.append(copy)
+            ch_copies[g, d] = copy
 
     def z_piece(j):
         return pl.ds(pl.multiple_of(j * piece, piece), piece) if split_z else pl.ds(0, piece)
 
     def plane_sum(g):
-        group = pl.ds(3 * g, 3)
+        group = pl.ds(*GROUPS[g])
         for d in range(1, ch_n):
-            ch_sends[g * (ch_n - 1) + d - 1].wait_recv()
+            ch_copies[g, d].wait_recv()
         acc = own[group, o_slice(chn), :]
         for d in range(1, ch_n):
             acc = acc + ch_r[d - 1, group].astype(F32)
@@ -264,12 +270,10 @@
                 zs_s.at[g, d - 1], zs_r.at[g, d - 1], 2 * z_at(d) + core, chn,
             )
             copy.start()
-            z_sends.append(copy)
-
-    ag_sends = []
+            sends.append(copy)
 
     def line_sum(g):
-        group = pl.ds(3 * g, 3)
+        group = pl.ds(*GROUPS[g])
         z_r[z, group] = z_s[group, z_piece(z), :]
         for d in range(1, zn):
             src = z_s.at[group, z_piece(z_at(d)), :]
@@ -285,21 +289,27 @@
                 copy = remote(mine, mine, ag_s.at[g, d - 1], ag_r.at[g, d - 1],
                               2 * z_at(d) + core, chn)
                 copy.start()
-                ag_sends.append(copy)
-
-    fin_sends = []
+                sends.append(copy)
 
     def pass_on(g):
-        group = pl.ds(3 * g, 3)
+        group = pl.ds(*GROUPS[g])
         if split_z:
+            mine = fin.at[core, group, z_piece(z), :]
             for d in range(1, zn):
                 theirs = fin.at[core, group, z_piece(z_from(d)), :]
-                remote(theirs, theirs, ag_s.at[g, d - 1], ag_r.at[g, d - 1],
+                remote(mine, theirs, ag_s.at[g, d - 1], ag_r.at[g, d - 1],
                        2 * z_at(d) + core, chn).wait_recv()
-        copy = remote(fin.at[core, group], fin.at[core, group],
-                      fn_s.at[g], fn_r.at[g], sib, chn)
+        both = fin.at[core, group]
+        copy = remote(both, both, fn_s.at[g], fn_r.at[g], sib, chn)
         copy.start()
-        fin_sends.append(copy)
+        sends.append(copy)
+
+    def finish(g):
+        group = pl.ds(*GROUPS[g])
+        remote(fin.at[core, group], fin.at[1 - core, group],
+               fn_s.at[g], fn_r.at[g], sib, chn).wait_recv()
+        w_grad[group, :, :LANES] = fin[0, group].astype(F32)
+        w_grad[group, :, LANES:] = fin[1, group].astype(F32)
 
     def transpose_taps(t, carry):
         r, c = t // 3, lax.rem(t, 3)
@@ -315,65 +325,51 @@
         shift_row(gs, s * (band + 1), after, before)
         return carry
 
-    out_copies = []
-
-    def input_row(h):
+    def input_row(h, carry):
         g_all = jnp.concatenate([gs[h], gs[h + 1], gs[h + 2]], axis=0)
-        ig[h] = jnp.dot(wt[...], g_all, preferred_element_type=F32).astype(BF16)
-
-    def input_out(h):
-        copy = pltpu.make_async_copy(ig.at[h], in_grad.at[h], out_sem.at[h])
-        copy.start()
-        out_copies.append(copy)
-
-    def input_edges(s, carry):
-        input_row(s * (band - 1))
-        return carry
-
-    def input_mid(s, carry):
-        input_row(s + 1)
-        return carry
-
-    weight_step(0)
-    weight_step(1)
-    combine(0)
-    weight_step(2)
-    combine(1)
-    lax.fori_loop(0, 9, transpose_taps, 0)
-    combine(2)
-    plane_sum(0)
-    lax.fori_loop(0, band, shift_g, 0)
-    plane_sum(1)
-    halo_finish(gs, g_up, g_dn)
-    lax.fori_loop(0, 2, shift_g_edge, 0)
-    plane_sum(2)
-    line_sum(0)
-    lax.fori_loop(0, band - 2, input_mid, 0)
+        in_grad[h] = jnp.dot(wt[...], g_all, preferred_element_type=F32).astype(BF16)
+        return carry
+
+    def edges_in():
+        halo_finish(gs, g_up, g_dn)
+        lax.fori_loop(0, 2, shift_g_edge, 0)
+
+    fill = [(0.3 * count, functools.partial(weight_step, g))
+            for g, (_, count) in enumerate(GROUPS)]
+    fill.append((0.8, lambda: lax.fori_loop(0, 9, transpose_taps, 0)))
+    fill.append((0.8, lambda: lax.fori_loop(0, band, shift_g, 0)))
     for h in range(1, band - 1):
-        input_out(h)
-    line_sum(1)
-    line_sum(2)
-    pass_on(0)
-    lax.fori_loop(0, 2, input_edges, 0)
+        fill.append((0.8, functools.partial(input_row, h, 0)))
+    fill.append((0.4, edges_in))
     for h in (0, band - 1):
-        input_out(h)
-    pass_on(1)
-    pass_on(2)
-    w_outs = []
-    for g in range(3):
-        group = pl.ds(3 * g, 3)
-        remote(fin.at[core, group], fin.at[1 - core, group],
-               fn_s.at[g], fn_r.at[g], sib, chn).wait_recv()
-        wout[group, :, :LANES] = fin[0, group].astype(F32)
-        wout[group, :, LANES:] = fin[1, group].astype(F32)
-        copy = pltpu.make_async_copy(wout.at[group], w_grad.at[group], out_sem.at[band + g])
-        copy.start()
-        w_outs.append(copy)
-
-    for copy in w_sends + f_sends + sib_copies + ch_sends + z_sends + ag_sends + fin_sends:
+        fill.append((0.8, functools.partial(input_row, h, 0)))
+    events = []
+    ready, wire = 0.0, 0.0
+    for g, (_, count) in enumerate(GROUPS):
+        ready = ready + 0.3 * count
+        at = ready + 0.5
+        events.append((at, g, combine))
+        wire = max(wire, at) + 0.7 * count
+        events.append((wire + 1.6, g, plane_sum))
+        events.append((wire + 6.0, g, line_sum))
+        events.append((wire + 10.4, g, pass_on))
+        events.append((wire + 11.8, g, finish))
+    events.sort(key=lambda e: e[:2])
+    now, done = 0.0, 0
+    while events or fill:
+        waits = events and events[0][2] is combine and events[0][1] >= done
+        if fill and (not events or waits or events[0][0] > now):
+            spent, step = fill.pop(0)
+            step()
+            done += 1
+            now += spent if done <= len(GROUPS) else spent * 1.0
+        else:
+            at, g, event = events.pop(0)
+            event(g)
+            now = max(now, at)
+
+    for copy in w_sends + f_sends + list(sib_copies.values()) + sends:
         copy.wait_send()
-    for copy in out_copies + w_outs:
-        copy.wait()
 
 
 def body(rows_n, ch_n, features, conv_weight, cotangent, valid_rows):
@@ -382,22 +378,22 @@
     zn = rows_n // 2
     split_z = part % (16 * zn) == 0
     piece = part // zn if split_z else part
+    groups = len(GROUPS)
     dma = pltpu.SemaphoreType.DMA
     anywhere = pl.BlockSpec(memory_space=pl.ANY)
     in_grad, w_grad = pl.pallas_call(
         functools.partial(kernel, rows_n, ch_n, split_z),
         out_shape=(
-            jax.ShapeDtypeStruct((band, total, cells), BF16),
-            jax.ShapeDtypeStruct((9, part, total), F32),
+            pltpu.VMEM((band, total, cells), BF16),
+            pltpu.VMEM((9, part, total), F32),
         ),
         in_specs=[anywhere, anywhere, anywhere, pl.BlockSpec(memory_space=pltpu.SMEM)],
-        out_specs=(anywhere, anywhere),
+        out_specs=(pl.BlockSpec(memory_space=pltpu.VMEM),) * 2,
         scratch_shapes=[
             pltpu.VMEM((band + 2, 3 * total, cells), BF16),
             pltpu.VMEM((band + 2, 3 * total, cells), BF16),
             pltpu.VMEM((9, total, total), BF16),
             pltpu.VMEM((total, 9 * total), BF16),
-            pltpu.VMEM((band, total, cells), BF16),
             pltpu.VMEM((band, total, cells), BF16),
             pltpu.VMEM((9, total, LANES), F32),
             pltpu.VMEM((9, total, LANES), BF16),
@@ -407,15 +403,14 @@
             pltpu.VMEM((9, part, LANES), BF16),
             pltpu.VMEM((zn, 9, piece, LANES), BF16),
             pltpu.VMEM((2, 9, part, LANES), BF16),
-            pltpu.VMEM((9, part, total), F32),
-            dma((3,)), dma((band + 3,)),
+            dma((3,)),
             dma((2,)), dma((2,)), dma((2,)), dma((2,)),
             dma((ch_n - 1,)), dma((ch_n - 1,)), dma((ch_n - 1,)), dma((ch_n - 1,)),
-            dma((3,)), dma((3,)),
-            dma((3, ch_n - 1)), dma((3, ch_n - 1)),
-            dma((3, zn - 1)), dma((3, zn - 1)),
-            dma((3, zn - 1)), dma((3, zn - 1)),
-            dma((3,)), dma((3,)),
+            dma((groups,)), dma((groups,)),
+            dma((groups, ch_n - 1)), dma((groups, ch_n - 1)),
+            dma((groups, zn - 1)), dma((groups, zn - 1)),
+            dma((groups, zn - 1)), dma((groups, zn - 1)),
+            dma((groups,)), dma((groups,)),
         ],
         compiler_params=pltpu.CompilerParams(
             collective_id=0, has_side_effects=True, vmem_limit_bytes=56 * 1024 * 1024

time: 45.4 us -> 43.5 us (0.958); the launches traced: 44.7 us -> 43.4 us
  local copies, waits for them, and re-layouts: 3.14 us -> 1.79 us
    unnamed x4 -> x2, local copies, waits for them, and re-layouts: 3.14 us -> 1.79 us
where the time goes in v2:
time: 43.5 us; the launch traced here: 43.4 us
  Pallas kernels  40.9 us (94%)
  local copies, waits for them, and re-layouts  1.79 us (4%)
  between operations  0.64 us (1%)
    pallas_call x1, Pallas kernels, body(): pl.pallas_call(functools.partial(kernel, rows_n, ch_n, split_z), out_shap...  40.9 us
    unnamed x2, local copies, waits for them, and re-layouts  1.79 us

profile of v2, /device:TPU:0, one launch (start us, length us, event | category | flops | bytes accessed | tf_op | source)
XLA Modules:
  0.0 43.4 jit_solution(10801770206643374124)
XLA Ops:
  0.6 40.9 %pyramid_backward.1 = (bf16[4,256,512]{2,1,0:T(8,128)(2,1)S(1)}, f32[9,64,256]{2,1,0:T(8,128)S(1)}) custom-call(bf16[4,256,512]{2,1,0:T(8,128)(2,1)} %feat.1, bf16[9,64,256]{2,1,0:T(8,128)(2,1)} %bitcast.3, bf16[4,256,512]{2,1,0:T(8,128)(2,1)} %cot.1, s32[16]{0:T(128)} %valid.1), custom_call_target="tpu_custom_call" | custom-call | tf_op jit(solution)/shard_map/pyramid_backward/pallas_call | solution.py:384
  41.6 1.0 %copy.8 = bf16[4,256,512]{2,1,0:T(8,128)(2,1)} copy(bf16[4,256,512]{2,1,0:T(8,128)(2,1)S(1)} %get-tuple-element.6) | data formatting | bytes 2097152
  42.6 0.8 %copy.9 = f32[3,3,64,256]{3,2,1,0:T(8,128)} copy(f32[3,3,64,256]{3,2,1,0:T(8,128)S(1)} %bitcast.2) | data formatting | bytes 1179648

commit v3 on v2

--- a/solution.py
+++ b/solution.py
@@ -59,9 +59,21 @@
     l_w = pltpu.make_async_copy(
         weight, wf.at[:, pl.ds(pl.multiple_of(chn * part, part), part), :], loc.at[2]
     )
-    l_feat.start()
-    l_w.start()
-    l_cot.start()
+    lane = lax.broadcasted_iota(jnp.int32, (total, COLS), 1)
+    before, after = 0, 2 * total
+
+    def shift_row(buf, p, minus_at, plus_at):
+        for n in range(imgs):
+            cols = pl.ds(n * COLS, COLS)
+            v = buf[p, total:2 * total, cols].astype(F32)
+            minus = jnp.where(lane == 0, 0.0, pltpu.roll(v, 1, 1))
+            plus = jnp.where(lane == COLS - 1, 0.0, pltpu.roll(v, COLS - 1, 1))
+            buf[p, minus_at:minus_at + total, cols] = minus.astype(BF16)
+            buf[p, plus_at:plus_at + total, cols] = plus.astype(BF16)
+
+    def shift_x(s, carry):
+        shift_row(xs, s + 1, before, after)
+        return carry
 
     barrier = pltpu.get_barrier_semaphore()
     for d in range(1, rows_n):
@@ -73,6 +85,11 @@
         pl.semaphore_signal(
             barrier, inc=1, device_id=(row, ch_at(d)), device_id_type=pl.DeviceIdType.MESH
         )
+    l_feat.start()
+    l_w.start()
+    l_cot.start()
+    l_feat.wait()
+    lax.fori_loop(0, band, shift_x, 0)
     pl.semaphore_wait(barrier, rows_n - 1 + ch_n - 1)
 
     half = pl.ds(pl.multiple_of(core * LANES, LANES), LANES)
@@ -133,25 +150,6 @@
 
     halo_start(x_up, x_dn)
 
-    lane = lax.broadcasted_iota(jnp.int32, (total, COLS), 1)
-    before, after = 0, 2 * total
-
-    def shift_row(buf, p, minus_at, plus_at):
-        for n in range(imgs):
-            cols = pl.ds(n * COLS, COLS)
-            v = buf[p, total:2 * total, cols].astype(F32)
-            minus = jnp.where(lane == 0, 0.0, pltpu.roll(v, 1, 1))
-            plus = jnp.where(lane == COLS - 1, 0.0, pltpu.roll(v, COLS - 1, 1))
-            buf[p, minus_at:minus_at + total, cols] = minus.astype(BF16)
-            buf[p, plus_at:plus_at + total, cols] = plus.astype(BF16)
-
-    l_feat.wait()
-
-    def shift_x(s, carry):
-        shift_row(xs, s + 1, before, after)
-        return carry
-
-    lax.fori_loop(0, band, shift_x, 0)
     halo_finish(xs, x_up, x_dn)
 
     def shift_x_edge(s, carry):

time: 43.5 us -> 43.2 us (level)
  no operation moved by 1% of the time
where the time goes in v3:
time: 43.2 us; the launch traced here: 43.1 us
  Pallas kernels  40.6 us (94%)
  local copies, waits for them, and re-layouts  1.79 us (4%)
  between operations  0.64 us (1%)
    pallas_call x1, Pallas kernels, body(): pl.pallas_call(functools.partial(kernel, rows_n, ch_n, split_z), out_shap...  40.6 us
    unnamed x2, local copies, waits for them, and re-layouts  1.79 us

profile of v3, /device:TPU:0, one launch (start us, length us, event | category | flops | bytes accessed | tf_op | source)
XLA Modules:
  0.0 43.1 jit_solution(1554868721748838429)
XLA Ops:
  0.6 40.6 %pyramid_backward.1 = (bf16[4,256,512]{2,1,0:T(8,128)(2,1)S(1)}, f32[9,64,256]{2,1,0:T(8,128)S(1)}) custom-call(bf16[4,256,512]{2,1,0:T(8,128)(2,1)} %feat.1, bf16[9,64,256]{2,1,0:T(8,128)(2,1)} %bitcast.3, bf16[4,256,512]{2,1,0:T(8,128)(2,1)} %cot.1, s32[16]{0:T(128)} %valid.1), custom_call_target="tpu_custom_call" | custom-call | tf_op jit(solution)/shard_map/pyramid_backward/pallas_call | solution.py:382
  41.3 1.0 %copy.8 = bf16[4,256,512]{2,1,0:T(8,128)(2,1)} copy(bf16[4,256,512]{2,1,0:T(8,128)(2,1)S(1)} %get-tuple-element.6) | data formatting | bytes 2097152
  42.3 0.8 %copy.9 = f32[3,3,64,256]{3,2,1,0:T(8,128)} copy(f32[3,3,64,256]{3,2,1,0:T(8,128)S(1)} %bitcast.2) | data formatting | bytes 1179648
